TPU v7x, 32 devices: a whole 2x2x4 slice. The times are simulated.
32 devices in a mesh: groups: 2 (over x), gx: 16 (over z, y, core).
Axes of the slice: x: 2, y: 2, z: 4, core: 2. Of those that a mesh axis runs over, the one named last changes fastest.
Arguments:
- positions: float32 [3, 131072], P(None, ('groups', 'gx')), parts along dimension 1, may hold values from -0.08 to 127.08, as said below
- radii: float32 [131072], P(('groups', 'gx')), parts along dimension 0, may hold values from 0.5 to 0.56
- neighbours: int32 [6, 131072], P(None, ('groups', 'gx')), parts along dimension 1, may hold values from 0 to 65535, as said below
- right_side: float32 [3, 131072], P(None, ('groups', 'gx')), parts along dimension 1, may hold values from -6 to 6
Outputs:
- solution_field: float32 [3, 131072], P(None, ('groups', 'gx')), parts along dimension 1
- residual: float32 [3, 131072], P(None, ('groups', 'gx')), parts along dimension 1
There are 2 independent parts, one for each index of `groups`. A program takes and returns all parts, laid end to end along the dimension named above; each array names one. Nothing has to cross between parts.
Inputs may be any that keep to these rules, and one draw needn't show every extreme that they name: `positions`: particles are ordered by lattice planes of 2048 along the first coordinate, rows of 128 within a plane; each lies within 0.08 of its lattice site in every coordinate. `neighbours`: each column lists distinct partners of the particle, the other slots hold the particle's own index; partnership is symmetric; every partner index is the particle's index plus or minus 1, 128 or 2048.
All inputs are finite; a program needn't handle non-finite values.
Results may differ from a plain program's by a relative error of at most 0.0003.
Values sent between devices are 32-bit elements; how exact they have to be, the bound alone decides.
A program may use at most 64 MiB of HBM per device.

v0:
```python
import jax
import jax.numpy as jnp
from jax import lax
from jax.sharding import PartitionSpec as P

LY = 16
LZ = 128
ITERS = 4


diagonal_shift = 4.0


def extended_2(array, sides, width):
    for axis, dim in sides:
        devices, length = (lax.axis_size(axis), array.shape[dim])
        up = [(i, (i + 1) % devices) for i in range(devices - 1)]
        down = [(j, i) for i, j in up]
        last = lax.slice_in_dim(array, length - width, length, axis=dim)
        first = lax.slice_in_dim(array, 0, width, axis=dim)
        before = lax.ppermute(last, axis, up)
        after = lax.ppermute(first, axis, down)
        array = jnp.concatenate([before, array, after], axis=dim)
    return array


def partner_values(extended, matches, offsets, owned, plane_size):
    own_view = extended[:, plane_size : plane_size + owned]
    partner = jnp.broadcast_to(
        own_view[:, None, :], (extended.shape[0], matches[0].shape[0], owned)
    )
    for which in range(len(offsets)):
        start = plane_size + offsets[which]
        view = extended[:, start : start + owned]
        partner = jnp.where(matches[which][None, :, :], view[:, None, :], partner)
    return partner


def pair_terms(own_geom, partner_geom, present):
    offset = partner_geom[:3] - own_geom[:3][:, None, :]
    squared = jnp.sum(offset * offset, axis=0)
    distance = jnp.sqrt(jnp.where(present, squared, jnp.float32(1.0)))
    normal = offset / distance
    contact = own_geom[3][None, :] + partner_geom[3]
    stiffness = 1.0 / (contact * contact)
    tension = -(1.0 - distance / contact) / (contact * distance)
    live_mask = present.astype(jnp.float32)
    return (normal, tension * live_mask, (stiffness - tension) * live_mask)


def apply_terms(vector, partner, blocks):
    normal, tension, radial = blocks
    relative = vector[:, None, :] - partner
    along_normal = jnp.sum(normal * relative, axis=0)
    return diagonal_shift * vector + jnp.sum(
        tension * relative + radial * normal * along_normal, axis=1
    )


def two_products(residual, image_vec):
    return lax.psum((jnp.sum(residual * residual), jnp.sum(residual * image_vec)), "gx")


def on_device(positions, radii, neighbours, right_side):
    owned = positions.shape[1]
    plane_size = LY * LZ
    first_id = lax.axis_index("gx") * owned
    own_ids = first_id + jnp.arange(owned, dtype=jnp.int32)
    present = neighbours != own_ids[None, :]
    offsets = [plane_size, -plane_size, LZ, -LZ, 1, -1]
    matches = [neighbours == (own_ids + shift_by)[None, :] for shift_by in offsets]
    geometry = jnp.concatenate([positions, radii[None, :]], axis=0)

    def operate(vector):
        joined = jnp.concatenate([geometry, vector], axis=0)
        extended = extended_2(joined, (("gx", 1),), plane_size)
        partner = partner_values(extended, matches, offsets, owned, plane_size)
        blocks = pair_terms(geometry, partner[:4], present)
        return apply_terms(vector, partner[4:], blocks)

    solution_field = jnp.zeros_like(right_side)
    residual = right_side
    image_vec = operate(residual)
    norm_now, product = two_products(residual, image_vec)
    step_size = norm_now / product
    direction = residual
    image_dir = image_vec
    for iteration in range(ITERS):
        solution_field = solution_field + step_size * direction
        residual = residual - step_size * image_dir
        if iteration + 1 < ITERS:
            image_vec = operate(residual)
            norm_next, product = two_products(residual, image_vec)
            beta_ratio = norm_next / norm_now
            step_size = norm_next / (product - beta_ratio * norm_next / step_size)
            direction = residual + beta_ratio * direction
            image_dir = image_vec + beta_ratio * image_dir
            norm_now = norm_next
    return (solution_field, residual)


def solution(mesh):
    return jax.shard_map(
        on_device,
        mesh=mesh,
        in_specs=(
            P(None, ("groups", "gx")),
            P(("groups", "gx")),
            P(None, ("groups", "gx")),
            P(None, ("groups", "gx")),
        ),
        out_specs=(P(None, ("groups", "gx")), P(None, ("groups", "gx"))),
        check_vma=False,
    )
```

profile of v0, /device:TPU:0, one launch (start us, length us, event | category | flops | bytes accessed | tf_op | source)
XLA Modules:
  0.0 172.8 jit_solution(15138034782257196625)
XLA Ops:
  0.6 0.9 pad_maximum_fusion.3
  1.6 2.5 %collective-permute-start = (f32[7,2048]{1,0:T(8,128)S(1)}, f32[7,2048]{1,0:T(8,128)S(1)}, u32[]{:S(2)}, u32[]{:S(2)}) collective-permute-start(f32[7,2048]{1,0:T(8,128)S(1)} %get-tuple-element.79), channel_id=1, source_target_pairs={{0,1},{1,2},{2,3},{3,4},{4,5},{5,6},{6,7},{7,8},{8,9},{9,10},{10,1... | collective-permute-start | bytes 172040 | tf_op jit(solution)/shard_map/ppermute | solution.py:21
  4.1 1.3 collective-permute-start.1
  5.7 3.7 %collective-permute-done.1 = f32[7,2048]{1,0:T(8,128)S(1)} collective-permute-done((f32[7,2048]{1,0:T(8,128)S(1)}, f32[7,2048]{1,0:T(8,128)S(1)}, u32[]{:S(2)}, u32[]{:S(2)}) %collective-permute-start.1) | collective-permute-done | bytes 57376 | tf_op jit(solution)/shard_map/ppermute | solution.py:22
  9.5 0.1 fusion.35
  9.6 0.3 select_select_fusion.3
  10.3 0.1 multiply_reduce_fusion.6
  10.4 0.3 add_reduce_fusion.3
  10.6 0.6 multiply_reduce_fusion.14
  11.3 33.3 %all-reduce.3 = (f32[]{:T(128)}, f32[]{:T(128)}) all-reduce(f32[]{:T(128)} %get-tuple-element.9, f32[]{:T(128)} %get-tuple-element.8), channel_id=1, replica_groups=mesh['groups'=2,'gx'=16] {'gx'}, use_global_device_ids=true, to_apply=%region_1.2 | all-reduce | flops 2 | bytes 16 | tf_op jit(solution)/shard_map/psum | solution.py:61
  46.1 1.3 collective-permute-start.2
  47.4 1.3 collective-permute-start.3
  48.7 1.8 %collective-permute-done.3 = f32[7,2048]{1,0:T(8,128)S(1)} collective-permute-done((f32[7,2048]{1,0:T(8,128)S(1)}, f32[7,2048]{1,0:T(8,128)S(1)}, u32[]{:S(2)}, u32[]{:S(2)}) %collective-permute-start.3) | collective-permute-done | bytes 57376 | tf_op jit(solution)/shard_map/ppermute | solution.py:22
  50.8 0.3 select_select_fusion.2
  51.5 0.3 add_reduce_fusion.2
  51.7 0.7 multiply_reduce_fusion.12
  52.4 31.3 %all-reduce.2 = (f32[]{:T(128)}, f32[]{:T(128)}) all-reduce(f32[]{:T(128)} %get-tuple-element.7, f32[]{:T(128)} %get-tuple-element.6), channel_id=1, replica_groups=mesh['groups'=2,'gx'=16] {'gx'}, use_global_device_ids=true, to_apply=%region_8.9 | all-reduce | flops 2 | bytes 16 | tf_op jit(solution)/shard_map/psum | solution.py:61
  88.5 1.3 collective-permute-start.4
  89.8 1.3 collective-permute-start.5
  91.1 1.8 %collective-permute-done.5 = f32[7,2048]{1,0:T(8,128)S(1)} collective-permute-done((f32[7,2048]{1,0:T(8,128)S(1)}, f32[7,2048]{1,0:T(8,128)S(1)}, u32[]{:S(2)}, u32[]{:S(2)}) %collective-permute-start.5) | collective-permute-done | bytes 57376 | tf_op jit(solution)/shard_map/ppermute | solution.py:22
  93.2 0.3 select_select_fusion.1
  93.8 0.3 add_reduce_fusion.1
  94.1 0.6 multiply_reduce_fusion.10
  94.7 31.9 %all-reduce.1 = (f32[]{:T(128)}, f32[]{:T(128)}) all-reduce(f32[]{:T(128)} %get-tuple-element.5, f32[]{:T(128)} %get-tuple-element.4), channel_id=1, replica_groups=mesh['groups'=2,'gx'=16] {'gx'}, use_global_device_ids=true, to_apply=%region_15.16 | all-reduce | flops 2 | bytes 16 | tf_op jit(solution)/shard_map/psum | solution.py:61
  130.7 1.3 collective-permute-start.6
  132.0 1.3 collective-permute-start.7
  133.3 1.8 %collective-permute-done.7 = f32[7,2048]{1,0:T(8,128)S(1)} collective-permute-done((f32[7,2048]{1,0:T(8,128)S(1)}, f32[7,2048]{1,0:T(8,128)S(1)}, u32[]{:S(2)}, u32[]{:S(2)}) %collective-permute-start.7) | collective-permute-done | bytes 57376 | tf_op jit(solution)/shard_map/ppermute | solution.py:22
  135.4 0.3 select_select_fusion
  136.0 0.3 add_reduce_fusion
  136.3 0.7 multiply_reduce_fusion.8
  137.0 31.3 %all-reduce = (f32[]{:T(128)}, f32[]{:T(128)}) all-reduce(f32[]{:T(128)} %get-tuple-element.3, f32[]{:T(128)} %get-tuple-element.2), channel_id=1, replica_groups=mesh['groups'=2,'gx'=16] {'gx'}, use_global_device_ids=true, to_apply=%region_22.23 | all-reduce | flops 2 | bytes 16 | tf_op jit(solution)/shard_map/psum | solution.py:61
  172.0 0.8 multiply_subtract_fusion
  (49 shorter events, 2.4 us)
Async XLA Ops:
  1.6 3.9 %copy-start.3 = (s32[6,4096]{1,0:T(8,128)S(1)}, s32[6,4096]{1,0:T(8,128)}, u32[]{:S(2)}) copy-start(s32[6,4096]{1,0:T(8,128)} %param.6) | copy-start | bytes 294916
  1.6 4.1 %collective-permute-start = (f32[7,2048]{1,0:T(8,128)S(1)}, f32[7,2048]{1,0:T(8,128)S(1)}, u32[]{:S(2)}, u32[]{:S(2)}) collective-permute-start(f32[7,2048]{1,0:T(8,128)S(1)} %get-tuple-element.79), channel_id=1, source_target_pairs={{0,1},{1,2},{2,3},{3,4},{4,5},{5,6},{6,7},{7,8},{8,9},{9,10},{10,1... | collective-permute-start | bytes 172040 | tf_op jit(solution)/shard_map/ppermute | solution.py:21
  4.1 5.3 %collective-permute-start.1 = (f32[7,2048]{1,0:T(8,128)S(1)}, f32[7,2048]{1,0:T(8,128)S(1)}, u32[]{:S(2)}, u32[]{:S(2)}) collective-permute-start(f32[7,2048]{1,0:T(8,128)S(1)} %get-tuple-element.80), channel_id=1, source_target_pairs={{1,0},{2,1},{3,2},{4,3},{5,4},{6,5},{7,6},{8,7},{9,8},{10,9},{11,1... | collective-permute-start | bytes 172040 | tf_op jit(solution)/shard_map/ppermute | solution.py:22
  5.5 3.9 %copy-start = (f32[3,4096]{1,0:T(4,128)S(1)}, f32[3,4096]{1,0:T(4,128)}, u32[]{:S(2)}) copy-start(f32[3,4096]{1,0:T(4,128)} %param.4) | copy-start | bytes 147460
  5.5 3.9 %copy-start.1 = (f32[3,4096]{1,0:T(4,128)S(1)}, f32[3,4096]{1,0:T(4,128)}, u32[]{:S(2)}) copy-start(f32[3,4096]{1,0:T(4,128)} %param.7) | copy-start | bytes 147460
  5.5 3.9 %copy-start.2 = (f32[4096]{0:T(1024)S(1)}, f32[4096]{0:T(1024)}, u32[]{:S(2)}) copy-start(f32[4096]{0:T(1024)} %param.5) | copy-start | bytes 49156
  46.1 2.6 %collective-permute-start.2 = (f32[7,2048]{1,0:T(8,128)S(1)}, f32[7,2048]{1,0:T(8,128)S(1)}, u32[]{:S(2)}, u32[]{:S(2)}) collective-permute-start(f32[7,2048]{1,0:T(8,128)S(1)} %get-tuple-element.71), channel_id=1, source_target_pairs={{0,1},{1,2},{2,3},{3,4},{4,5},{5,6},{6,7},{7,8},{8,9},{9,10},{10,1... | collective-permute-start | bytes 172040 | tf_op jit(solution)/shard_map/ppermute | solution.py:21
  47.4 3.1 %collective-permute-start.3 = (f32[7,2048]{1,0:T(8,128)S(1)}, f32[7,2048]{1,0:T(8,128)S(1)}, u32[]{:S(2)}, u32[]{:S(2)}) collective-permute-start(f32[7,2048]{1,0:T(8,128)S(1)} %get-tuple-element.72), channel_id=1, source_target_pairs={{1,0},{2,1},{3,2},{4,3},{5,4},{6,5},{7,6},{8,7},{9,8},{10,9},{11,1... | collective-permute-start | bytes 172040 | tf_op jit(solution)/shard_map/ppermute | solution.py:22
  88.5 2.6 %collective-permute-start.4 = (f32[7,2048]{1,0:T(8,128)S(1)}, f32[7,2048]{1,0:T(8,128)S(1)}, u32[]{:S(2)}, u32[]{:S(2)}) collective-permute-start(f32[7,2048]{1,0:T(8,128)S(1)} %get-tuple-element.69), channel_id=1, source_target_pairs={{0,1},{1,2},{2,3},{3,4},{4,5},{5,6},{6,7},{7,8},{8,9},{9,10},{10,1... | collective-permute-start | bytes 172040 | tf_op jit(solution)/shard_map/ppermute | solution.py:21
  89.8 3.1 %collective-permute-start.5 = (f32[7,2048]{1,0:T(8,128)S(1)}, f32[7,2048]{1,0:T(8,128)S(1)}, u32[]{:S(2)}, u32[]{:S(2)}) collective-permute-start(f32[7,2048]{1,0:T(8,128)S(1)} %get-tuple-element.70), channel_id=1, source_target_pairs={{1,0},{2,1},{3,2},{4,3},{5,4},{6,5},{7,6},{8,7},{9,8},{10,9},{11,1... | collective-permute-start | bytes 172040 | tf_op jit(solution)/shard_map/ppermute | solution.py:22
  130.7 2.6 %collective-permute-start.6 = (f32[7,2048]{1,0:T(8,128)S(1)}, f32[7,2048]{1,0:T(8,128)S(1)}, u32[]{:S(2)}, u32[]{:S(2)}) collective-permute-start(f32[7,2048]{1,0:T(8,128)S(1)} %get-tuple-element.67), channel_id=1, source_target_pairs={{0,1},{1,2},{2,3},{3,4},{4,5},{5,6},{6,7},{7,8},{8,9},{9,10},{10,1... | collective-permute-start | bytes 172040 | tf_op jit(solution)/shard_map/ppermute | solution.py:21
  132.0 3.1 %collective-permute-start.7 = (f32[7,2048]{1,0:T(8,128)S(1)}, f32[7,2048]{1,0:T(8,128)S(1)}, u32[]{:S(2)}, u32[]{:S(2)}) collective-permute-start(f32[7,2048]{1,0:T(8,128)S(1)} %get-tuple-element.68), channel_id=1, source_target_pairs={{1,0},{2,1},{3,2},{4,3},{5,4},{6,5},{7,6},{8,7},{9,8},{10,9},{11,1... | collective-permute-start | bytes 172040 | tf_op jit(solution)/shard_map/ppermute | solution.py:22
where the time goes:
time: 173 us
  blocking collectives  128 us (74%)
  between operations  14.6 us (8%)
  starting transfers between devices  11.6 us (7%)
  waiting for transfers between devices  9.26 us (5%)
  other arithmetic  8.76 us (5%)
    psum x4, blocking collectives, two_products(): lax.psum((jnp.sum(residual * residual), jnp.sum(residual * image_vec)), '...  128 us
    ppermute x4, waiting for transfers between devices, extended_2(): after = lax.ppermute(first, axis, down)  9.25 us
    ppermute x4, starting transfers between devices, extended_2(): before = lax.ppermute(last, axis, up)  6.41 us
    ppermute x4, starting transfers between devices, extended_2(): after = lax.ppermute(first, axis, down)  5.17 us
  transfers between devices with their start and end apart: 8, of which 4 were waited for; matrix products, arithmetic and copies ran while one was open for 0% of the time, Pallas kernels for 0%

commit v1 on v0

v1 whole, which is shorter than its diff:
```python
import jax
import jax.numpy as jnp
from jax import lax
from jax.sharding import PartitionSpec as P

LY = 16
LZ = 128
ITERS = 4


diagonal_shift = 4.0


def with_halo(array, width):
    devices, length = (lax.axis_size("gx"), array.shape[1])
    up = [(i, i + 1) for i in range(devices - 1)]
    down = [(j, i) for i, j in up]
    before = lax.ppermute(array[:, length - width :], "gx", up)
    after = lax.ppermute(array[:, :width], "gx", down)
    return jnp.concatenate([before, array, after], axis=1)


def partners(extended, rows):
    def view(start):
        return extended[:, start : start + rows]

    own = view(LY)
    return [
        view(2 * LY),
        view(0),
        view(LY + 1),
        view(LY - 1),
        jnp.concatenate([own[:, :, 1:], view(LY + 1)[:, :, :1]], axis=2),
        jnp.concatenate([view(LY - 1)[:, :, LZ - 1 :], own[:, :, : LZ - 1]], axis=2),
    ]


def pair_terms(own_geom, partner_geom, present):
    offset = partner_geom[:3] - own_geom[:3]
    squared = jnp.sum(offset * offset, axis=0)
    distance = jnp.sqrt(jnp.where(present, squared, jnp.float32(1.0)))
    normal = jnp.where(present[None], offset, 0.0) / distance
    contact = jnp.where(present, own_geom[3] + partner_geom[3], jnp.float32(1.0))
    stiffness = 1.0 / (contact * contact)
    tension = -(1.0 - distance / contact) / (contact * distance)
    live_mask = present.astype(jnp.float32)
    return (normal, tension * live_mask, (stiffness - tension) * live_mask)


def apply_terms(vector, partner, blocks):
    image = diagonal_shift * vector
    for value, (normal, tension, radial) in zip(partner, blocks):
        relative = vector - value
        along = radial * jnp.sum(normal * relative, axis=0)
        image = image + (tension * relative + normal * along)
    return image


def two_products(residual, image_vec):
    return lax.psum((jnp.sum(residual * residual), jnp.sum(residual * image_vec)), "gx")


def on_device(positions, radii, neighbours, right_side):
    owned = positions.shape[1]
    rows = owned // LZ
    shape = right_side.shape
    first_id = lax.axis_index("gx") * owned
    own_ids = (first_id + jnp.arange(owned, dtype=jnp.int32)).reshape(rows, LZ)
    neighbours = neighbours.reshape(-1, rows, LZ)
    offsets = [LY * LZ, -LY * LZ, LZ, -LZ, 1, -1]
    present = [jnp.any(neighbours == own_ids + by, axis=0) for by in offsets]
    geometry = jnp.concatenate([positions, radii[None, :]], axis=0)
    geometry = geometry.reshape(4, rows, LZ)
    right_side = right_side.reshape(3, rows, LZ)
    joined = with_halo(jnp.concatenate([geometry, right_side], axis=0), LY)
    first = partners(joined, rows)
    blocks = [pair_terms(geometry, f[:4], here) for f, here in zip(first, present)]
    blocks = lax.optimization_barrier(blocks)

    def operate(vector):
        return apply_terms(vector, partners(with_halo(vector, LY), rows), blocks)

    solution_field = jnp.zeros_like(right_side)
    residual = right_side
    image_vec = apply_terms(residual, [f[4:] for f in first], blocks)
    norm_now, product = two_products(residual, image_vec)
    step_size = norm_now / product
    direction = residual
    image_dir = image_vec
    for iteration in range(ITERS):
        solution_field = solution_field + step_size * direction
        residual = residual - step_size * image_dir
        if iteration + 1 < ITERS:
            image_vec = operate(residual)
            norm_next, product = two_products(residual, image_vec)
            beta_ratio = norm_next / norm_now
            step_size = norm_next / (product - beta_ratio * norm_next / step_size)
            direction = residual + beta_ratio * direction
            image_dir = image_vec + beta_ratio * image_dir
            norm_now = norm_next
    return (solution_field.reshape(shape), residual.reshape(shape))


def solution(mesh):
    return jax.shard_map(
        on_device,
        mesh=mesh,
        in_specs=(
            P(None, ("groups", "gx")),
            P(("groups", "gx")),
            P(None, ("groups", "gx")),
            P(None, ("groups", "gx")),
        ),
        out_specs=(P(None, ("groups", "gx")), P(None, ("groups", "gx"))),
        check_vma=False,
    )
```

time: 173 us -> 172 us (level)
  waiting for transfers between devices: 9.26 us -> 2.14 us
  starting transfers between devices: 11.6 us -> 17.3 us
  local copies, waits for them, and re-layouts: 0.78 us -> 3.97 us
  other arithmetic: 8.76 us -> 6.2 us
    ppermute x8, waiting for transfers between devices: 9.26 us -> 2.14 us  [the longest x4 2.13 us: with_halo(): before = lax.ppermute(array[:, length - width:], 'gx', up)]
    ppermute x8, starting transfers between devices: 11.6 us -> 17.3 us  [the longest x4 12.1 us: with_halo(): before = lax.ppermute(array[:, length - width:], 'gx', up)]
    unnamed x8, local copies, waits for them, and re-layouts: 0.03 us -> 2.64 us
  transfers between devices with their start and end apart: 8 -> 8, of which waited for: 4 -> 3; matrix products, arithmetic and copies ran while one was open for 0% -> 1% of each run, Pallas kernels for 0% -> 0%
where the time goes in v1:
time: 172 us
  blocking collectives  127 us (74%)
  starting transfers between devices  17.3 us (10%)
  between operations  15 us (9%)
  other arithmetic  6.2 us (4%)
  local copies, waits for them, and re-layouts  3.97 us (2%)
  waiting for transfers between devices  2.14 us (1%)
    psum x4, blocking collectives, two_products(): lax.psum((jnp.sum(residual * residual), jnp.sum(residual * image_vec)), '...  127 us
    ppermute x4, starting transfers between devices, with_halo(): before = lax.ppermute(array[:, length - width:], 'gx', up)  12.1 us
    ppermute x4, starting transfers between devices, with_halo(): after = lax.ppermute(array[:, :width], 'gx', down)  5.16 us
  transfers between devices with their start and end apart: 8, of which 3 were waited for; matrix products, arithmetic and copies ran while one was open for 1% of the time, Pallas kernels for 0%

profile of v1, /device:TPU:0, one launch (start us, length us, event | category | flops | bytes accessed | tf_op | source)
XLA Modules:
  0.0 171.7 jit_solution(18012722133856649220)
XLA Ops:
  0.6 0.9 copy_bitcast_fusion.2
  1.6 1.3 collective-permute-start
  2.9 3.0 %collective-permute-start.1 = (f32[7,16,128]{2,1,0:T(8,128)S(1)}, f32[7,16,128]{2,1,0:T(8,128)S(1)}, u32[]{:S(2)}, u32[]{:S(2)}) collective-permute-start(f32[7,16,128]{2,1,0:T(8,128)S(1)} %get-tuple-element.131), channel_id=1, source_target_pairs={{0,1},{1,2},{2,3},{3,4},{4,5},{5,6},{6,7},{7,8},{8,9},{9,10},{10,1... | collective-permute-start | bytes 172040 | tf_op jit(solution)/shard_map/ppermute | solution.py:18
  6.1 0.7 copy-done.2
  6.8 0.3 compare_reduce_fusion
  7.1 0.6 copy-done.1
  7.7 0.6 multiply_reduce_fusion
  8.4 0.1 multiply_reduce_fusion.32
  8.9 0.1 select_divide_fusion
  9.0 0.1 multiply_reduce_fusion.31
  9.2 0.7 multiply_reduce_fusion.25
  9.9 35.1 %all-reduce.3 = (f32[]{:T(128)}, f32[]{:T(128)}) all-reduce(f32[]{:T(128)} %multiply_reduce_fusion, f32[]{:T(128)} %get-tuple-element.98), channel_id=1, replica_groups=mesh['groups'=2,'gx'=16] {'gx'}, use_global_device_ids=true, to_apply=%region_1.0 | all-reduce | flops 2 | bytes 16 | tf_op jit(solution)/shard_map/psum | solution.py:60
  46.4 1.3 collective-permute-start.2
  47.8 3.0 %collective-permute-start.3 = (f32[3,16,128]{2,1,0:T(8,128)S(1)}, f32[3,16,128]{2,1,0:T(8,128)S(1)}, u32[]{:S(2)}, u32[]{:S(2)}) collective-permute-start(f32[3,16,128]{2,1,0:T(8,128)S(1)} %get-tuple-element.151), channel_id=1, source_target_pairs={{0,1},{1,2},{2,3},{3,4},{4,5},{5,6},{6,7},{7,8},{8,9},{9,10},{10,1... | collective-permute-start | bytes 73736 | tf_op jit(solution)/shard_map/ppermute | solution.py:18
  50.9 0.7 collective-permute-done.3
  51.8 0.8 multiply_reduce_fusion.17
  52.6 30.5 %all-reduce.2 = (f32[]{:T(128)}, f32[]{:T(128)}) all-reduce(f32[]{:T(128)} %get-tuple-element.67, f32[]{:T(128)} %get-tuple-element.66), channel_id=1, replica_groups=mesh['groups'=2,'gx'=16] {'gx'}, use_global_device_ids=true, to_apply=%region_23.24 | all-reduce | flops 2 | bytes 16 | tf_op jit(solution)/shard_map/psum | solution.py:60
  87.7 1.3 collective-permute-start.4
  89.1 3.0 %collective-permute-start.5 = (f32[3,16,128]{2,1,0:T(8,128)S(1)}, f32[3,16,128]{2,1,0:T(8,128)S(1)}, u32[]{:S(2)}, u32[]{:S(2)}) collective-permute-start(f32[3,16,128]{2,1,0:T(8,128)S(1)} %get-tuple-element.147), channel_id=1, source_target_pairs={{0,1},{1,2},{2,3},{3,4},{4,5},{5,6},{6,7},{7,8},{8,9},{9,10},{10,1... | collective-permute-start | bytes 73736 | tf_op jit(solution)/shard_map/ppermute | solution.py:18
  92.3 0.7 collective-permute-done.5
  93.0 0.1 multiply_reduce_fusion.14
  93.1 0.7 multiply_reduce_fusion.9
  93.9 31.0 %all-reduce.1 = (f32[]{:T(128)}, f32[]{:T(128)}) all-reduce(f32[]{:T(128)} %get-tuple-element.47, f32[]{:T(128)} %get-tuple-element.46), channel_id=1, replica_groups=mesh['groups'=2,'gx'=16] {'gx'}, use_global_device_ids=true, to_apply=%region_33.34 | all-reduce | flops 2 | bytes 16 | tf_op jit(solution)/shard_map/psum | solution.py:60
  128.8 0.6 multiply_subtract_fusion
  129.4 1.3 collective-permute-start.6
  130.8 3.0 %collective-permute-start.7 = (f32[3,16,128]{2,1,0:T(8,128)S(1)}, f32[3,16,128]{2,1,0:T(8,128)S(1)}, u32[]{:S(2)}, u32[]{:S(2)}) collective-permute-start(f32[3,16,128]{2,1,0:T(8,128)S(1)} %get-tuple-element.143), channel_id=1, source_target_pairs={{0,1},{1,2},{2,3},{3,4},{4,5},{5,6},{6,7},{7,8},{8,9},{9,10},{10,1... | collective-permute-start | bytes 73736 | tf_op jit(solution)/shard_map/ppermute | solution.py:18
  133.9 0.7 collective-permute-done.7
  134.8 0.8 multiply_reduce_fusion.1
  135.6 30.5 %all-reduce = (f32[]{:T(128)}, f32[]{:T(128)}) all-reduce(f32[]{:T(128)} %get-tuple-element.121, f32[]{:T(128)} %multiply_reduce_fusion.1), channel_id=1, replica_groups=mesh['groups'=2,'gx'=16] {'gx'}, use_global_device_ids=true, to_apply=%region_43.44 | all-reduce | flops 2 | bytes 16 | tf_op jit(solution)/shard_map/psum | solution.py:60
  170.2 0.1 subtract_bitcast_fusion
  170.3 0.7 copy.14
  171.0 0.7 copy.15
  (63 shorter events, 1.5 us)
Async XLA Ops:
  0.6 0.9 copy-start
  1.6 6.7 %collective-permute-start = (f32[7,16,128]{2,1,0:T(8,128)S(1)}, f32[7,16,128]{2,1,0:T(8,128)S(1)}, u32[]{:S(2)}, u32[]{:S(2)}) collective-permute-start(f32[7,16,128]{2,1,0:T(8,128)S(1)} %get-tuple-element.130), channel_id=1, source_target_pairs={{1,0},{2,1},{3,2},{4,3},{5,4},{6,5},{7,6},{8,7},{9,8},{10,9},{11,1... | collective-permute-start | bytes 172040 | tf_op jit(solution)/shard_map/ppermute | solution.py:19
  2.9 5.4 %collective-permute-start.1 = (f32[7,16,128]{2,1,0:T(8,128)S(1)}, f32[7,16,128]{2,1,0:T(8,128)S(1)}, u32[]{:S(2)}, u32[]{:S(2)}) collective-permute-start(f32[7,16,128]{2,1,0:T(8,128)S(1)} %get-tuple-element.131), channel_id=1, source_target_pairs={{0,1},{1,2},{2,3},{3,4},{4,5},{5,6},{6,7},{7,8},{8,9},{9,10},{10,1... | collective-permute-start | bytes 172040 | tf_op jit(solution)/shard_map/ppermute | solution.py:18
  5.9 0.9 copy-start.2
  6.8 0.8 copy-start.1
  46.4 4.4 %collective-permute-start.2 = (f32[3,16,128]{2,1,0:T(8,128)S(1)}, f32[3,16,128]{2,1,0:T(8,128)S(1)}, u32[]{:S(2)}, u32[]{:S(2)}) collective-permute-start(f32[3,16,128]{2,1,0:T(8,128)S(1)} %get-tuple-element.150), channel_id=1, source_target_pairs={{1,0},{2,1},{3,2},{4,3},{5,4},{6,5},{7,6},{8,7},{9,8},{10,9},{11,1... | collective-permute-start | bytes 73736 | tf_op jit(solution)/shard_map/ppermute | solution.py:19
  47.8 3.9 %collective-permute-start.3 = (f32[3,16,128]{2,1,0:T(8,128)S(1)}, f32[3,16,128]{2,1,0:T(8,128)S(1)}, u32[]{:S(2)}, u32[]{:S(2)}) collective-permute-start(f32[3,16,128]{2,1,0:T(8,128)S(1)} %get-tuple-element.151), channel_id=1, source_target_pairs={{0,1},{1,2},{2,3},{3,4},{4,5},{5,6},{6,7},{7,8},{8,9},{9,10},{10,1... | collective-permute-start | bytes 73736 | tf_op jit(solution)/shard_map/ppermute | solution.py:18
  87.7 4.4 %collective-permute-start.4 = (f32[3,16,128]{2,1,0:T(8,128)S(1)}, f32[3,16,128]{2,1,0:T(8,128)S(1)}, u32[]{:S(2)}, u32[]{:S(2)}) collective-permute-start(f32[3,16,128]{2,1,0:T(8,128)S(1)} %get-tuple-element.146), channel_id=1, source_target_pairs={{1,0},{2,1},{3,2},{4,3},{5,4},{6,5},{7,6},{8,7},{9,8},{10,9},{11,1... | collective-permute-start | bytes 73736 | tf_op jit(solution)/shard_map/ppermute | solution.py:19
  89.1 3.9 %collective-permute-start.5 = (f32[3,16,128]{2,1,0:T(8,128)S(1)}, f32[3,16,128]{2,1,0:T(8,128)S(1)}, u32[]{:S(2)}, u32[]{:S(2)}) collective-permute-start(f32[3,16,128]{2,1,0:T(8,128)S(1)} %get-tuple-element.147), channel_id=1, source_target_pairs={{0,1},{1,2},{2,3},{3,4},{4,5},{5,6},{6,7},{7,8},{8,9},{9,10},{10,1... | collective-permute-start | bytes 73736 | tf_op jit(solution)/shard_map/ppermute | solution.py:18
  129.4 4.4 %collective-permute-start.6 = (f32[3,16,128]{2,1,0:T(8,128)S(1)}, f32[3,16,128]{2,1,0:T(8,128)S(1)}, u32[]{:S(2)}, u32[]{:S(2)}) collective-permute-start(f32[3,16,128]{2,1,0:T(8,128)S(1)} %get-tuple-element.142), channel_id=1, source_target_pairs={{1,0},{2,1},{3,2},{4,3},{5,4},{6,5},{7,6},{8,7},{9,8},{10,9},{11,1... | collective-permute-start | bytes 73736 | tf_op jit(solution)/shard_map/ppermute | solution.py:19
  130.8 3.9 %collective-permute-start.7 = (f32[3,16,128]{2,1,0:T(8,128)S(1)}, f32[3,16,128]{2,1,0:T(8,128)S(1)}, u32[]{:S(2)}, u32[]{:S(2)}) collective-permute-start(f32[3,16,128]{2,1,0:T(8,128)S(1)} %get-tuple-element.143), channel_id=1, source_target_pairs={{0,1},{1,2},{2,3},{3,4},{4,5},{5,6},{6,7},{7,8},{8,9},{9,10},{10,1... | collective-permute-start | bytes 73736 | tf_op jit(solution)/shard_map/ppermute | solution.py:18
